TPU v7x, 32 devices: a whole 2x2x4 slice. The times are simulated.
32 devices in a mesh: seq: 8 (over z, x), head: 4 (over y, core).
Axes of the slice: x: 2, y: 2, z: 4, core: 2. Of those that a mesh axis runs over, the one named last changes fastest.
Arguments:
- query_rows: bfloat16 [16384, 1024], P('seq', 'head'), may hold values from -8 to 8
- key_rows: bfloat16 [16384, 1024], P('seq', 'head'), may hold values from -6 to 6
- value_rows: bfloat16 [16384, 1024], P('seq', 'head'), may hold values from -12 to 12
- out_grad: bfloat16 [16384, 1024], P('seq', 'head'), may hold values from -12 to 12
- block_perm: int32 [8, 64], P('head'), may hold values from 0 to 63, as said below
- cut_count: int32 [8], P('head'), may hold values from 1 to 4, as said below
- norm_gain: float32 [1024], P('head'), may hold values from 0.1 to 1.9
Outputs:
- normed_out: bfloat16 [16384, 1024], P('seq', 'head')
- query_grad: bfloat16 [16384, 1024], P('seq', 'head')
- key_grad: bfloat16 [16384, 1024], P('seq', 'head')
- value_grad: bfloat16 [16384, 1024], P('seq', 'head')
- gain_grad: float32 [1024], P('head')
Inputs may be any that keep to these rules, and one draw needn't show every extreme that they name: `block_perm`: each row is a permutation of 0 to 63. For every head, of the 8 blocks d * 8 to (d + 1) * 8 - 1, at most 1 are paired with blocks of one range s * 8 to (s + 1) * 8 - 1, and some pair (d, s) reaches 1. `cut_count`: some head has exactly 4.
All inputs are finite; a program needn't handle non-finite values.
Results may differ from a plain program's by a relative error of at most 0.0071.
Values may be sent and summed in bfloat16 or wider, within the bound.
A program may use at most 128 MiB of HBM per device.

v0:
```python
from functools import partial
import jax
import jax.numpy as jnp
from jax import lax
from jax.sharding import PartitionSpec as P

BLOCK = 256
KCUT = 4


def split_heads(rows, heads):
    tokens = rows.shape[0]
    width = rows.shape[1] // heads
    return rows.reshape(tokens // BLOCK, BLOCK, heads, width).transpose(2, 0, 1, 3)


def merge_heads(parts):
    return parts.transpose(1, 2, 0, 3).reshape(
        parts.shape[1] * parts.shape[2], parts.shape[0] * parts.shape[3]
    )


def to_slots(rows, slot_of, count):
    match = slot_of[:, None, :] == jnp.arange(count)[None, :, None]
    chosen = jnp.sum(jnp.where(match, jnp.arange(rows.shape[1])[None, None, :], 0), axis=2)
    filled = jnp.any(match, axis=2)
    picked = jax.vmap(lambda piece, which: piece[which])(rows, chosen)
    shape = filled.shape + (1,) * (rows.ndim - 2)
    return jnp.where(filled.reshape(shape), picked, jnp.zeros_like(picked))


def from_slots(slot_rows, slot_of):
    return jax.vmap(lambda piece, which: piece[which])(slot_rows, slot_of)


def attend(query, own_rows, paired_rows, cutoff_rows, live, scale):
    width = query.shape[-1]
    span = own_rows.shape[1]
    count = cutoff_rows.shape[0]
    own = jnp.einsum(
        "gqd,gkd->gqk", query, own_rows[..., :width], preferred_element_type=jnp.float32
    )
    pair = jnp.einsum(
        "gqd,gkd->gqk", query, paired_rows[..., :width], preferred_element_type=jnp.float32
    )
    cut = jnp.einsum(
        "gqd,ckd->gqck", query, cutoff_rows[..., :width], preferred_element_type=jnp.float32
    )
    cut = cut.reshape(query.shape[0], query.shape[1], count * span)
    scores = jnp.concatenate([own, pair, cut], axis=-1) * scale
    open_keys = jnp.concatenate([jnp.ones((2 * span,), jnp.bool_), jnp.repeat(live, span)])
    scores = jnp.where(open_keys, scores, -1e30)
    top = jnp.max(scores, axis=-1)
    weights = jnp.exp(scores - top[..., None])
    total = jnp.sum(weights, axis=-1)
    return (weights / total[..., None], top, total)


def forward_head(query, own_rows, paired_rows, cutoff_rows, live, scale):
    width = query.shape[-1]
    span = query.shape[1]
    groups = query.shape[0] // 2
    count = cutoff_rows.shape[0]

    def forward_step(pieces):
        query_part, own_part, pair_part = pieces
        prob, top, total = attend(query_part, own_part, pair_part, cutoff_rows, live, scale)
        weights = prob.astype(jnp.bfloat16)
        result = jnp.einsum(
            "gqk,gkd->gqd",
            weights[..., :span],
            own_part[..., width:],
            preferred_element_type=jnp.float32,
        )
        result = result + jnp.einsum(
            "gqk,gkd->gqd",
            weights[..., span : 2 * span],
            pair_part[..., width:],
            preferred_element_type=jnp.float32,
        )
        cut_weight = weights[..., 2 * span :].reshape(2, span, count, span)
        result = result + jnp.einsum(
            "gqck,ckd->gqd",
            cut_weight,
            cutoff_rows[..., width:],
            preferred_element_type=jnp.float32,
        )
        return result.astype(jnp.bfloat16)

    result = lax.map(
        forward_step,
        (
            query.reshape(groups, 2, span, width),
            own_rows.reshape(groups, 2, span, 2 * width),
            paired_rows.reshape(groups, 2, span, 2 * width),
        ),
    )
    return result.reshape(query.shape)


def backward_head(query, own_rows, paired_rows, cutoff_rows, live, cotangent, scale):
    width = query.shape[-1]
    span = query.shape[1]
    groups = query.shape[0] // 2
    count = cutoff_rows.shape[0]

    def backward_step(carry, pieces):
        query_part, own_part, pair_part, cot_part = pieces
        prob, top, total = attend(query_part, own_part, pair_part, cutoff_rows, live, scale)
        weights = prob.astype(jnp.bfloat16)
        dprob = jnp.concatenate(
            [
                jnp.einsum(
                    "gqd,gkd->gqk",
                    cot_part,
                    own_part[..., width:],
                    preferred_element_type=jnp.float32,
                ),
                jnp.einsum(
                    "gqd,gkd->gqk",
                    cot_part,
                    pair_part[..., width:],
                    preferred_element_type=jnp.float32,
                ),
                jnp.einsum(
                    "gqd,ckd->gqck",
                    cot_part,
                    cutoff_rows[..., width:],
                    preferred_element_type=jnp.float32,
                ).reshape(2, span, count * span),
            ],
            axis=-1,
        )
        delta = jnp.sum(prob * dprob, axis=-1)
        dscore = (prob * (dprob - delta[..., None]) * scale).astype(jnp.bfloat16)
        cut_score = dscore[..., 2 * span :].reshape(2, span, count, span)
        cut_weight = weights[..., 2 * span :].reshape(2, span, count, span)
        query_grad = jnp.einsum(
            "gqk,gkd->gqd",
            dscore[..., :span],
            own_part[..., :width],
            preferred_element_type=jnp.float32,
        )
        query_grad = query_grad + jnp.einsum(
            "gqk,gkd->gqd",
            dscore[..., span : 2 * span],
            pair_part[..., :width],
            preferred_element_type=jnp.float32,
        )
        query_grad = query_grad + jnp.einsum(
            "gqck,ckd->gqd", cut_score, cutoff_rows[..., :width], preferred_element_type=jnp.float32
        )
        own_grad = jnp.concatenate(
            [
                jnp.einsum(
                    "gqk,gqd->gkd",
                    dscore[..., :span],
                    query_part,
                    preferred_element_type=jnp.float32,
                ),
                jnp.einsum(
                    "gqk,gqd->gkd",
                    weights[..., :span],
                    cot_part,
                    preferred_element_type=jnp.float32,
                ),
            ],
            axis=-1,
        )
        pair_grad = jnp.concatenate(
            [
                jnp.einsum(
                    "gqk,gqd->gkd",
                    dscore[..., span : 2 * span],
                    query_part,
                    preferred_element_type=jnp.float32,
                ),
                jnp.einsum(
                    "gqk,gqd->gkd",
                    weights[..., span : 2 * span],
                    cot_part,
                    preferred_element_type=jnp.float32,
                ),
            ],
            axis=-1,
        )
        cut_grad = jnp.concatenate(
            [
                jnp.einsum(
                    "gqck,gqd->ckd", cut_score, query_part, preferred_element_type=jnp.float32
                ),
                jnp.einsum(
                    "gqck,gqd->ckd", cut_weight, cot_part, preferred_element_type=jnp.float32
                ),
            ],
            axis=-1,
        )
        return (
            carry + cut_grad,
            (query_grad.astype(jnp.bfloat16), own_grad, pair_grad, top, total, delta),
        )

    start = jnp.zeros((count, span, 2 * width), jnp.float32)
    cut_sum, outputs = lax.scan(
        backward_step,
        start,
        (
            query.reshape(groups, 2, span, width),
            own_rows.reshape(groups, 2, span, 2 * width),
            paired_rows.reshape(groups, 2, span, 2 * width),
            cotangent.reshape(groups, 2, span, width),
        ),
    )
    query_grad, own_grad, pair_grad, top, total, delta = outputs
    blocks = query.shape[0]
    return (
        query_grad.reshape(query.shape),
        own_grad.reshape(own_rows.shape),
        pair_grad.reshape(own_rows.shape),
        cut_sum,
        top.reshape(blocks, span),
        total.reshape(blocks, span),
        delta.reshape(blocks, span),
    )


def owner_pair(query, cotangent, top, total, delta, own_rows, scale):
    width = query.shape[-1]
    scores = (
        jnp.einsum("jqd,jkd->jqk", query, own_rows[..., :width], preferred_element_type=jnp.float32)
        * scale
    )
    prob = jnp.exp(scores - top[..., None]) / total[..., None]
    dprob = jnp.einsum(
        "jqd,jkd->jqk", cotangent, own_rows[..., width:], preferred_element_type=jnp.float32
    )
    dscore = (prob * (dprob - delta[..., None]) * scale).astype(jnp.bfloat16)
    return jnp.concatenate(
        [
            jnp.einsum("jqk,jqd->jkd", dscore, query, preferred_element_type=jnp.float32),
            jnp.einsum(
                "jqk,jqd->jkd",
                prob.astype(jnp.bfloat16),
                cotangent,
                preferred_element_type=jnp.float32,
            ),
        ],
        axis=-1,
    )


def body(query_rows, key_rows, value_rows, out_grad, block_perm, cut_count, norm_gain):
    heads = block_perm.shape[0]
    width = query_rows.shape[1] // heads
    blocks = query_rows.shape[0] // BLOCK
    seq_count = lax.axis_size("seq")
    head_count = lax.axis_size("head")
    capacity = (blocks + seq_count - 1) // seq_count
    slot_count = seq_count * capacity
    scale = width ** (-0.5)
    position = lax.axis_index("seq")
    query_h = split_heads(query_rows, heads)
    grad_h = split_heads(out_grad, heads)
    own_rows = jnp.concatenate(
        [split_heads(key_rows, heads), split_heads(value_rows, heads)], axis=-1
    )
    local_perm = lax.dynamic_slice_in_dim(block_perm, position * blocks, blocks, 1)
    source_dev = local_perm // blocks
    lower = jnp.arange(blocks)[:, None] > jnp.arange(blocks)[None, :]
    same_source = source_dev[:, :, None] == source_dev[:, None, :]
    recv_slot = source_dev * capacity + jnp.sum(same_source & lower[None], axis=2)
    owned = position * blocks + jnp.arange(blocks)
    hits = block_perm[:, None, :] == owned[None, :, None]
    dest_global = jnp.sum(
        jnp.where(hits, jnp.arange(block_perm.shape[1])[None, None, :], 0), axis=2
    )
    dest_dev = dest_global // blocks
    dest_local = dest_global % blocks
    before = (dest_dev[:, :, None] == dest_dev[:, None, :]) & (
        dest_local[:, None, :] < dest_local[:, :, None]
    )
    send_slot = dest_dev * capacity + jnp.sum(before, axis=2)
    own_send = to_slots(own_rows, send_slot, slot_count)
    query_send = to_slots(query_h, recv_slot, slot_count)
    own_recv, query_recv = (
        lax.all_to_all(own_send, "seq", split_axis=1, concat_axis=1, tiled=True),
        lax.all_to_all(query_send, "seq", split_axis=1, concat_axis=1, tiled=True),
    )
    query_owner = from_slots(query_recv, send_slot)
    paired_rows = from_slots(own_recv, recv_slot)
    cut_global = block_perm[:, :KCUT]
    cut_dev = cut_global // blocks
    cut_local = cut_global % blocks
    cut_pick = jax.vmap(lambda piece, which: piece[which])(own_rows, cut_local)
    cut_pick = jnp.where(
        (cut_dev == position)[:, :, None, None], cut_pick, jnp.zeros_like(cut_pick)
    )
    cutoff_rows = lax.psum(cut_pick.astype(jnp.float32).astype(jnp.bfloat16), "seq")
    live = jnp.arange(KCUT)[None, :] < cut_count[:, None]
    attn = jax.vmap(partial(forward_head, scale=scale))(
        query_h, own_rows, paired_rows, cutoff_rows, live
    )
    attn_f = attn.astype(jnp.float32)
    grad_f = grad_h.astype(jnp.float32)
    gain = norm_gain.reshape(heads, 1, 1, width)
    square_part = jnp.sum(attn_f * attn_f, axis=(0, 3))
    mix_part = jnp.sum(gain * grad_f * attn_f, axis=(0, 3))
    square_sum, mix_sum = lax.psum((square_part, mix_part), "head")
    features = head_count * heads * width
    scale_row = lax.rsqrt(square_sum / features + 1e-06)[None, :, :, None]
    normed = (attn_f * scale_row * gain).astype(jnp.bfloat16)
    gain_part = jnp.sum(grad_f * attn_f * scale_row, axis=(1, 2))
    cotangent = (
        scale_row * gain * grad_f - attn_f * scale_row**3 * mix_sum[None, :, :, None] / features
    ).astype(jnp.bfloat16)
    query_grad, own_grad, pair_grad, cut_grad, top, total, delta = jax.vmap(
        partial(backward_head, scale=scale)
    )(query_h, own_rows, paired_rows, cutoff_rows, live, cotangent)
    cot_send = to_slots(cotangent, recv_slot, slot_count)
    cot_recv = lax.all_to_all(cot_send, "seq", split_axis=1, concat_axis=1, tiled=True)
    top_send = to_slots(top, recv_slot, slot_count)
    total_send = to_slots(total, recv_slot, slot_count)
    delta_send = to_slots(delta, recv_slot, slot_count)
    top_recv, total_recv, delta_recv = (
        lax.all_to_all(top_send, "seq", split_axis=1, concat_axis=1, tiled=True),
        lax.all_to_all(total_send, "seq", split_axis=1, concat_axis=1, tiled=True),
        lax.all_to_all(delta_send, "seq", split_axis=1, concat_axis=1, tiled=True),
    )
    pair_full = jax.vmap(partial(owner_pair, scale=scale))(
        query_owner,
        from_slots(cot_recv, send_slot),
        from_slots(top_recv, send_slot),
        from_slots(total_recv, send_slot),
        from_slots(delta_recv, send_slot),
        own_rows,
    )
    pair_term = lax.optimization_barrier(pair_full.astype(jnp.bfloat16)).astype(jnp.float32)
    cut_total, gain_total = lax.psum((cut_grad, gain_part), "seq")
    match = (
        (cut_dev == position)[:, :, None]
        & (cut_local[:, :, None] == jnp.arange(blocks)[None, None, :])
    ).astype(jnp.float32)
    cut_term = jnp.einsum("hcj,hcqd->hjqd", match, cut_total, precision=lax.Precision.HIGHEST)
    total_grad = (own_grad + pair_term + cut_term).astype(jnp.bfloat16)
    return (
        merge_heads(normed),
        merge_heads(query_grad),
        merge_heads(total_grad[..., :width]),
        merge_heads(total_grad[..., width:]),
        gain_total.reshape(heads * width),
    )


def solution(mesh):
    placed = (
        P("seq", "head"),
        P("seq", "head"),
        P("seq", "head"),
        P("seq", "head"),
        P("head", None),
        P("head"),
        P("head"),
    )
    return jax.shard_map(
        body,
        mesh=mesh,
        in_specs=placed,
        out_specs=(
            P("seq", "head"),
            P("seq", "head"),
            P("seq", "head"),
            P("seq", "head"),
            P("head"),
        ),
        check_vma=False,
    )
```

profile of v0, /device:TPU:0, one launch (start us, length us, event | category | flops | bytes accessed | tf_op | source)
XLA Modules:
  0.0 683.0 jit_solution(10543006544791201384)
XLA Ops:
  15.9 3.1 copy_select_fusion
  19.0 7.3 %all-to-all-start = ((bf16[2,8,256,256]{3,2,0,1:T(8,128)(2,1)}), bf16[2,8,256,256]{3,2,0,1:T(8,128)(2,1)}, u32[]{:S(2)}, u32[]{:S(2)}) async-start(bf16[2,8,256,256]{3,2,0,1:T(8,128)(2,1)} %copy_select_fusion), calls=%async_computation | async-start | bytes 4194304 | tf_op jit(solution)/shard_map/all_to_all | solution.py:286
  36.0 51.3 %all-to-all-done = bf16[2,8,256,256]{3,2,0,1:T(8,128)(2,1)} async-done(((bf16[2,8,256,256]{3,2,0,1:T(8,128)(2,1)}), bf16[2,8,256,256]{3,2,0,1:T(8,128)(2,1)}, u32[]{:S(2)}, u32[]{:S(2)}) %all-to-all-start) | async-done | bytes 2097184 | tf_op jit(solution)/shard_map/all_to_all | solution.py:286
  91.1 3.1 copy.276
  94.2 40.7 %all-reduce.5.cloned.1.call-done = bf16[2,4,256,256]{3,2,1,0:T(8,128)(2,1)} async-done(((bf16[2,4,256,256]{3,2,1,0:T(8,128)(2,1)}), bf16[2,4,256,256]{3,2,1,0:T(8,128)(2,1)}) %all-reduce.5.cloned.1.call-update) | async-done | bytes 1048592 | tf_op jit(solution)/shard_map/psum | solution.py:298
  136.1 76.6 %while.32 = (s32[]{:T(128)}, bf16[4,2,2,256,128]{4,3,2,0,1:T(8,128)(2,1)}, bf16[4,2,2,256,128]{4,3,2,1,0:T(8,128)(2,1)S(1)}, bf16[4,2,2,256,256]{4,3,2,1,0:T(8,1...) while((s32[]{:T(128)}, ...), condition=%wide.region_9.10_spmd.clone, body=%wide.region_6.9_spmd.clone.sunk | while | flops 818284032 | bytes 55597728 | solution.py:90
  142.7 5.4 copy.414
  148.3 3.7 fusion.235
  161.8 5.4 copy.414
  167.4 3.7 fusion.235
  181.0 5.4 copy.414
  186.6 3.7 fusion.235
  200.1 5.4 copy.414
  205.7 3.7 fusion.235
  217.2 6.9 %psum.36 = f32[8,256]{1,0:T(8,128)S(1)} all-reduce(f32[8,256]{1,0:T(8,128)S(1)} %reduce_sum.131), channel_id=1, replica_groups=mesh['seq'=8,'head'=4] {'head'}, use_global_device_ids=true, to_apply=%region_11.12 | all-reduce | flops 2048 | bytes 16384 | tf_op jit(solution)/shard_map/psum | solution.py:308
  227.0 6.3 psum.37
  233.3 3.2 fusion.113
  237.7 237.2 %while.33 = (s32[]{:T(128)}, f32[2,4,256,256]{2,3,1,0:T(8,128)}, bf16[4,2,2,256,128]{4,3,2,0,1:T(8,128)(2,1)}, f32[4,2,2,256,256]{3,4,2,1,0:T(8,128)}, f32[4,2,2...) while((s32[]{:T(128)}, f32[2,4,256,256]{2,3,1,0:T(8,128)}, ...), condition=%wide.region_18.19_spmd.clone, body=%wide.region_14.18_spmd.clone.sunk | while | flops 1934750720 | bytes 244144336 | solution.py:204
  243.4 5.4 copy.417
  258.1 5.4 copy.416
  263.5 5.6 multiply_reduce_fusion.3
  302.2 5.4 copy.417
  316.8 5.4 copy.416
  322.2 5.6 multiply_reduce_fusion.3
  352.4 3.5 maximum_add_fusion.2
  361.7 5.4 copy.417
  376.3 5.4 copy.416
  381.7 5.6 multiply_reduce_fusion.3
  411.9 3.5 maximum_add_fusion.2
  421.1 5.4 copy.417
  435.8 5.4 copy.416
  441.2 5.6 multiply_reduce_fusion.3
  471.4 3.5 maximum_add_fusion.2
  477.6 9.9 %all_to_all.30 = f32[2,8,256]{2,0,1:T(2,128)S(1)} all-to-all(f32[2,8,256]{2,0,1:T(2,128)S(1)} %get-tuple-element.372), channel_id=1, replica_groups=mesh['seq'=8,'head'=4] {'seq'}, dimensions={1} | all-to-all | bytes 32768 | tf_op jit(solution)/shard_map/all_to_all | solution.py:325
  487.5 3.3 all-to-all-start.3
  492.8 2.9 gather_fusion.9
  497.3 4.3 all-to-all-start.5
  501.6 3.0 copy_select_fusion.2
  504.6 3.6 all-to-all-done.5
  508.2 26.6 %all_to_all.31 = bf16[2,8,256,128]{3,2,0,1:T(8,128)(2,1)} all-to-all(bf16[2,8,256,128]{3,2,0,1:T(8,128)(2,1)} %get-tuple-element.373), channel_id=1, replica_groups=mesh['seq'=8,'head'=4] {'seq'}, dimensions={1} | all-to-all | bytes 2097152 | tf_op jit(solution)/shard_map/all_to_all | solution.py:287
  534.8 3.7 all-to-all-start.4
  540.5 4.6 copy.287
  549.6 28.1 %psum.39 = f32[256]{0:T(256)} all-reduce(f32[256]{0:T(256)S(1)} %bitcast.413), channel_id=1, replica_groups=mesh['seq'=8,'head'=4] {'seq'}, use_global_device_ids=true, to_apply=%region_23.24 | all-reduce | flops 256 | bytes 2048 | tf_op jit(solution)/shard_map/psum | solution.py:338
  587.4 4.8 fusion.121
  593.5 63.7 %all-reduce.7.cloned.1.call-done = f32[2,4,256,256]{3,1,2,0:T(4,128)} async-done(((f32[2,4,256,256]{3,1,2,0:T(4,128)}), f32[2,4,256,256]{3,1,2,0:T(4,128)}) %all-reduce.7.cloned.1.call-update) | async-done | bytes 2097168 | tf_op jit(solution)/shard_map/psum | solution.py:338
  657.2 5.3 fusion.130
  662.5 5.3 copy.306
  667.8 4.4 add_convert_fusion
  (454 shorter events, 259.1 us)
Async XLA Ops:
  15.9 10.5 %copy-start.31 = (s32[2,64]{1,0:T(2,128)S(1)}, s32[2,64]{1,0:T(2,128)}, u32[]{:S(2)}) copy-start(s32[2,64]{1,0:T(2,128)} %param.15) | copy-start | bytes 1540
  19.0 68.4 %all-to-all-start = ((bf16[2,8,256,256]{3,2,0,1:T(8,128)(2,1)}), bf16[2,8,256,256]{3,2,0,1:T(8,128)(2,1)}, u32[]{:S(2)}, u32[]{:S(2)}) async-start(bf16[2,8,256,256]{3,2,0,1:T(8,128)(2,1)} %copy_select_fusion), calls=%async_computation | async-start | bytes 4194304 | tf_op jit(solution)/shard_map/all_to_all | solution.py:286
  26.3 108.6 %all-reduce.5.cloned.1.call-start = ((), (), s32[]{:S(2)}) async-start(), calls=%async_computation.6 | async-start | bytes 2097152 | tf_op jit(solution)/shard_map/psum | solution.py:298
  89.1 47.0 %copy-start.42 = (s32[2]{0:T(128)S(1)}, s32[2]{0:T(128)}, u32[]{:S(2)}) copy-start(s32[2]{0:T(128)} %param.16) | copy-start | bytes 28
  212.7 11.5 %copy-start.19 = (f32[8,256,2,128]{3,2,1,0:T(2,128)S(1)}, f32[8,256,2,128]{3,2,1,0:T(2,128)}, u32[]{:S(2)}) copy-start(f32[8,256,2,128]{3,2,1,0:T(2,128)} %reshape.418) | copy-start | bytes 6291460
  212.7 11.5 %copy-start.41 = (f32[256]{0:T(256)S(1)}, f32[256]{0:T(256)}, u32[]{:S(2)}) copy-start(f32[256]{0:T(256)} %param.17) | copy-start | bytes 3076
  237.7 237.3 %copy-start.28 = (s32[16]{0:T(128)S(1)}, s32[16]{0:T(128)}, u32[]{:S(2)}) copy-start(s32[16]{0:T(128)} %reshape.321) | copy-start | bytes 196
  237.7 239.1 %copy-start.39 = (pred[2,8]{0,1:T(8,128)(4,1)S(1)}, pred[2,8]{0,1:T(8,128)(4,1)}, u32[]{:S(2)}) copy-start(pred[2,8]{0,1:T(8,128)(4,1)} %copy.288) | copy-start | bytes 52
  237.7 5.7 copy-start.7
  263.5 5.6 copy-start.1
  263.5 6.2 copy-start.2
  263.5 6.4 copy-start.6
  280.8 5.7 copy-start.8
  282.9 5.5 copy-start.5
  296.5 5.7 copy-start.7
  322.2 5.6 copy-start.1
  322.2 6.2 copy-start.2
  322.2 6.4 copy-start.6
  331.1 4.0 copy-start.3
  331.1 4.0 copy-start.4
  339.6 5.7 copy-start.8
  341.7 5.5 copy-start.5
  356.0 5.7 copy-start.7
  381.7 5.6 copy-start.1
  381.7 6.2 copy-start.2
  381.7 6.4 copy-start.6
  399.0 5.7 copy-start.8
  401.1 5.5 copy-start.5
  415.4 5.7 copy-start.7
  441.2 5.6 copy-start.1
  441.2 6.2 copy-start.2
  441.2 6.4 copy-start.6
  450.0 4.0 copy-start.3
  450.1 4.0 copy-start.4
  458.5 5.7 copy-start.8
  460.6 5.5 copy-start.5
  487.5 9.8 %all-to-all-start.3 = ((f32[2,8,256]{2,0,1:T(2,128)}), f32[2,8,256]{2,0,1:T(2,128)S(1)}, u32[]{:S(2)}, u32[]{:S(2)}) async-start(f32[2,8,256]{2,0,1:T(2,128)} %get-tuple-element.371), calls=%async_computation.3 | async-start | bytes 32768 | tf_op jit(solution)/shard_map/all_to_all | solution.py:326
  497.3 10.9 %all-to-all-start.5 = ((f32[2,8,256]{2,0,1:T(2,128)}), f32[2,8,256]{2,0,1:T(2,128)S(1)}, u32[]{:S(2)}, u32[]{:S(2)}) async-start(f32[2,8,256]{2,0,1:T(2,128)} %get-tuple-element.370), calls=%async_computation.5 | async-start | bytes 32768 | tf_op jit(solution)/shard_map/all_to_all | solution.py:327
  501.6 36.9 %copy-start.17 = (f32[2,4,256,256]{2,3,1,0:T(8,128)S(1)}, f32[2,4,256,256]{2,3,1,0:T(8,128)}, u32[]{:S(2)}) copy-start(f32[2,4,256,256]{2,3,1,0:T(8,128)} %get-tuple-element.120) | copy-start | bytes 6291460
  534.8 5.7 copy-start.34
  534.8 5.7 copy-start.36
  534.8 46.5 %all-to-all-start.4 = ((bf16[2,8,256,128]{3,2,0,1:T(8,128)(2,1)}), bf16[2,8,256,128]{3,2,0,1:T(8,128)(2,1)S(1)}, u32[]{:S(2)}, u32[]{:S(2)}) async-start(bf16[2,8,256,128]{3,2,0,1:T(8,128)(2,1)} %get-tuple-element.374), calls=%async_computation.4 | async-start | bytes 2097152 | tf_op jit(solution)/shard_map/all_to_all | solution.py:320
  538.5 118.7 %all-reduce.7.cloned.1.call-start = ((), (), s32[]{:S(2)}) async-start(), calls=%async_computation.7 | async-start | bytes 4194304 | tf_op jit(solution)/shard_map/psum | solution.py:338
  540.5 4.7 copy-start.25
  545.2 4.4 copy-start.40
  545.2 34.3 %copy-start.24 = (bf16[2,8,256,128]{3,2,0,1:T(8,128)(2,1)S(1)}, bf16[2,8,256,128]{3,2,0,1:T(8,128)(2,1)}, u32[]{:S(2)}) copy-start(bf16[2,8,256,128]{3,2,0,1:T(8,128)(2,1)} %all_to_all.31) | copy-start | bytes 3145732
  592.1 65.1 %copy-start.32 = (s32[2,4]{1,0:T(2,128)S(1)}, s32[2,4]{1,0:T(2,128)}, u32[]{:S(2)}) copy-start(s32[2,4]{1,0:T(2,128)} %get-tuple-element.351) | copy-start | bytes 100
  592.1 65.1 %copy-start.38 = (pred[2,4]{1,0:T(4,128)(4,1)S(1)}, pred[2,4]{1,0:T(4,128)(4,1)}, u32[]{:S(2)}) copy-start(pred[2,4]{1,0:T(4,128)(4,1)} %copy-done.37) | copy-start | bytes 28
  (55 other events, 128.4 us)
Sparse Core Ops, SparseCore 0:
  31.2 103.6 all-reduce.4
  542.9 114.2 all-reduce.6
where the time goes:
time: 686 us; the launch traced here: 683 us
  local copies, waits for them, and re-layouts  173 us (25%)
  waiting for transfers between devices  161 us (23%)
  matrix products  123 us (18%)
  other arithmetic  114 us (17%)
  blocking collectives  77.8 us (11%)
  starting transfers between devices  18.7 us (3%)
  between operations  14.6 us (2%)
    psum x1, waiting for transfers between devices, body(): cut_total, gain_total = lax.psum((cut_grad, gain_part), 'seq')  63.7 us
    all_to_all x1, waiting for transfers between devices, body(): lax.all_to_all(own_send, 'seq', split_axis=1, concat_axis=1, tiled=True)  51.3 us
    reshape x8, local copies, waits for them, and re-layouts, attend(): cut = cut.reshape(query.shape[0], query.shape[1], count * span)  43.2 us
    psum x1, waiting for transfers between devices, body(): lax.psum(cut_pick.astype(jnp.float32).astype(jnp.bfloat16), 'seq')  40.7 us
    psum x1, blocking collectives, body(): cut_total, gain_total = lax.psum((cut_grad, gain_part), 'seq')  28.1 us
    all_to_all x1, blocking collectives, body(): lax.all_to_all(query_send, 'seq', split_axis=1, concat_axis=1, tiled=True)  26.6 us
    reduce_sum x4, other arithmetic, backward_step(): delta = jnp.sum(prob * dprob, axis=-1)  22.4 us
    reshape x4, local copies, waits for them, and re-layouts, backward_step(): dprob = jnp.concatenate([jnp.einsum('gqd,gkd->gqk', cot_part, own_part[.....  21.7 us
  transfers between devices with their start and end apart: 6, of which 5 were waited for; matrix products, arithmetic and copies ran while one was open for 7% of the time, Pallas kernels for 0%

commit v1 on v0

--- a/solution.py
+++ b/solution.py
@@ -295,7 +295,9 @@
     cut_pick = jnp.where(
         (cut_dev == position)[:, :, None, None], cut_pick, jnp.zeros_like(cut_pick)
     )
-    cutoff_rows = lax.psum(cut_pick.astype(jnp.float32).astype(jnp.bfloat16), "seq")
+    cutoff_rows = jnp.sum(
+        lax.all_gather(cut_pick.astype(jnp.float32).astype(jnp.bfloat16), "seq"), axis=0
+    )
     live = jnp.arange(KCUT)[None, :] < cut_count[:, None]
     attn = jax.vmap(partial(forward_head, scale=scale))(
         query_h, own_rows, paired_rows, cutoff_rows, live

time: 686 us -> 747 us (1.089)
  waiting for transfers between devices: 161 us -> 202 us
  matrix products: 123 us -> 135 us
    all_gather x0 -> x1, waiting for transfers between devices: none -> 61.6 us  [body(): lax.all_gather(cut_pick.astype(jnp.float32).astype(jnp.bfloat16), 'seq')]
    psum x1 -> x0, waiting for transfers between devices: 40.7 us -> none  [body(): lax.psum(cut_pick.astype(jnp.float32).astype(jnp.bfloat16), 'seq')]
    all_to_all x1, waiting for transfers between devices: 51.3 us -> 72.2 us  [body(): lax.all_to_all(own_send, 'seq', split_axis=1, concat_axis=1, tiled=True)]
    unnamed x61 -> x57, local copies, waits for them, and re-layouts: 17 us -> 16.4 us
where the time goes in v1:
time: 747 us; the launch traced here: 744 us
  waiting for transfers between devices  202 us (27%)
  local copies, waits for them, and re-layouts  179 us (24%)
  matrix products  135 us (18%)
  other arithmetic  117 us (16%)
  blocking collectives  77.7 us (10%)
  starting transfers between devices  18.7 us (3%)
  between operations  14.6 us (2%)
    all_to_all x1, waiting for transfers between devices, body(): lax.all_to_all(own_send, 'seq', split_axis=1, concat_axis=1, tiled=True)  72.2 us
    psum x1, waiting for transfers between devices, body(): cut_total, gain_total = lax.psum((cut_grad, gain_part), 'seq')  62.5 us
    all_gather x1, waiting for transfers between devices, body(): lax.all_gather(cut_pick.astype(jnp.float32).astype(jnp.bfloat16), 'seq')  61.6 us
    reshape x8, local copies, waits for them, and re-layouts, attend(): cut = cut.reshape(query.shape[0], query.shape[1], count * span)  43.3 us
    psum x1, blocking collectives, body(): cut_total, gain_total = lax.psum((cut_grad, gain_part), 'seq')  28.7 us
    all_to_all x1, blocking collectives, body(): lax.all_to_all(query_send, 'seq', split_axis=1, concat_axis=1, tiled=True)  26.8 us
    dot_general x8, matrix products, attend(): jnp.einsum('gqd,ckd->gqck', query, cutoff_rows[..., :width], preferred_el...  25.2 us
    reshape x4, local copies, waits for them, and re-layouts, backward_step(): dprob = jnp.concatenate([jnp.einsum('gqd,gkd->gqk', cot_part, own_part[.....  21.6 us
  transfers between devices with their start and end apart: 6, of which 5 were waited for; matrix products, arithmetic and copies ran while one was open for 7% of the time, Pallas kernels for 0%

profile of v1, /device:TPU:0, one launch (start us, length us, event | category | flops | bytes accessed | tf_op | source)
XLA Modules:
  0.0 743.7 jit_solution(10740071549612117477)
XLA Ops:
  20.3 7.3 all-to-all-start
  35.9 72.2 %all-to-all-done = bf16[2,8,256,256]{3,2,0,1:T(8,128)(2,1)} async-done(((bf16[2,8,256,256]{3,2,0,1:T(8,128)(2,1)}), bf16[2,8,256,256]{3,2,0,1:T(8,128)(2,1)}, u32[]{:S(2)}, u32[]{:S(2)}) %all-to-all-start) | async-done | bytes 2097184 | tf_op jit(solution)/shard_map/all_to_all | solution.py:286
  117.8 61.6 %all-gather.2.cloned.1.call-done = bf16[8,2,4,256,256]{4,3,2,1,0:T(8,128)(2,1)} async-done(((bf16[1,2,4,256,256]{4,3,2,1,0:T(8,128)(2,1)}), bf16[8,2,4,256,256]{4,3,2,1,0:T(8,128)(2,1)}) %all-gather.2.cloned.1.call-update) | async-done | bytes 8388624 | tf_op jit(solution)/shard_map/all_gather | solution.py:299
  179.4 5.0 reduce_sum.142
  185.6 76.1 %while.32 = (s32[]{:T(128)}, bf16[4,2,2,256,128]{4,3,2,0,1:T(8,128)(2,1)}, bf16[4,2,2,256,128]{4,3,2,1,0:T(8,128)(2,1)S(1)}, bf16[4,2,2,256,256]{4,3,2,1,0:T(8,1...) while((s32[]{:T(128)}, ...), condition=%wide.region_9.10_spmd.clone, body=%wide.region_6.9_spmd.clone.sunk | while | flops 818284032 | bytes 51403396 | solution.py:90
  192.1 5.4 copy.414
  197.7 3.7 fusion.235
  211.1 5.4 copy.414
  216.7 3.7 fusion.235
  230.2 5.4 copy.414
  235.7 3.7 fusion.235
  249.2 5.4 copy.414
  254.8 3.7 fusion.235
  266.1 5.9 psum.28
  275.5 6.6 psum.29
  282.2 3.7 fusion.113
  287.0 249.2 %while.33 = (s32[]{:T(128)}, f32[2,4,256,256]{2,3,1,0:T(8,128)}, bf16[4,2,2,256,128]{4,3,2,0,1:T(8,128)(2,1)}, f32[4,2,2,256,256]{3,4,2,1,0:T(8,128)}, f32[4,2,2...) while((s32[]{:T(128)}, f32[2,4,256,256]{2,3,1,0:T(8,128)}, ...), condition=%wide.region_18.19_spmd.clone, body=%wide.region_14.18_spmd.clone.sunk | while | flops 1934750720 | bytes 244146352 | solution.py:204
  291.1 3.6 fusion.268
  294.7 5.4 copy.417
  306.8 3.7 fusion.265
  310.4 5.4 copy.416
  315.8 5.1 multiply_reduce_fusion.3
  356.6 5.4 copy.417
  368.6 3.7 fusion.265
  372.3 5.4 copy.416
  377.7 5.1 multiply_reduce_fusion.3
  415.4 3.6 fusion.268
  419.0 5.4 copy.417
  431.0 3.7 fusion.265
  434.7 5.4 copy.416
  440.1 5.1 multiply_reduce_fusion.3
  477.8 3.6 fusion.268
  481.4 5.4 copy.417
  493.5 3.7 fusion.265
  497.1 5.4 copy.416
  502.5 5.1 multiply_reduce_fusion.3
  538.8 9.6 %all_to_all.30 = f32[2,8,256]{2,0,1:T(2,128)S(1)} all-to-all(f32[2,8,256]{2,0,1:T(2,128)S(1)} %get-tuple-element.372), channel_id=1, replica_groups=mesh['seq'=8,'head'=4] {'seq'}, dimensions={1} | all-to-all | bytes 32768 | tf_op jit(solution)/shard_map/all_to_all | solution.py:327
  558.3 4.3 all-to-all-start.5
  565.4 3.7 all-to-all-done.5
  569.1 26.8 %all_to_all.31 = bf16[2,8,256,128]{3,2,0,1:T(8,128)(2,1)} all-to-all(bf16[2,8,256,128]{3,2,0,1:T(8,128)(2,1)} %get-tuple-element.373), channel_id=1, replica_groups=mesh['seq'=8,'head'=4] {'seq'}, dimensions={1} | all-to-all | bytes 2097152 | tf_op jit(solution)/shard_map/all_to_all | solution.py:287
  595.9 3.7 all-to-all-start.4
  601.7 4.6 copy.286
  610.7 28.7 %psum.31 = f32[256]{0:T(256)} all-reduce(f32[256]{0:T(256)S(1)} %bitcast.413), channel_id=1, replica_groups=mesh['seq'=8,'head'=4] {'seq'}, use_global_device_ids=true, to_apply=%region_23.24 | all-reduce | flops 256 | bytes 2048 | tf_op jit(solution)/shard_map/psum | solution.py:340
  649.2 4.8 fusion.121
  655.4 62.5 %all-reduce.4.cloned.1.call-done = f32[2,4,256,256]{3,1,2,0:T(4,128)} async-done(((f32[2,4,256,256]{3,1,2,0:T(4,128)}), f32[2,4,256,256]{3,1,2,0:T(4,128)}) %all-reduce.4.cloned.1.call-update) | async-done | bytes 2097168 | tf_op jit(solution)/shard_map/psum | solution.py:340
  717.9 5.3 fusion.130
  723.3 5.3 copy.305
  728.5 4.4 add_convert_fusion
  (443 shorter events, 276.2 us)
Async XLA Ops:
  7.2 172.3 %all-gather.2.cloned.1.call-start = ((), (), s32[]{:S(2)}) async-start(), calls=%async_computation.6 | async-start | bytes 9437184 | tf_op jit(solution)/shard_map/all_gather | solution.py:299
  14.6 5.7 copy-start.30
  20.3 87.8 %all-to-all-start = ((bf16[2,8,256,256]{3,2,0,1:T(8,128)(2,1)}), bf16[2,8,256,256]{3,2,0,1:T(8,128)(2,1)}, u32[]{:S(2)}, u32[]{:S(2)}) async-start(bf16[2,8,256,256]{3,2,0,1:T(8,128)(2,1)} %copy_select_fusion), calls=%async_computation | async-start | bytes 4194304 | tf_op jit(solution)/shard_map/all_to_all | solution.py:286
  117.8 67.8 %copy-start.39 = (s32[2]{0:T(128)S(1)}, s32[2]{0:T(128)}, u32[]{:S(2)}) copy-start(s32[2]{0:T(128)} %param.16) | copy-start | bytes 28
  261.7 10.3 %copy-start.38 = (f32[256]{0:T(256)S(1)}, f32[256]{0:T(256)}, u32[]{:S(2)}) copy-start(f32[256]{0:T(256)} %param.17) | copy-start | bytes 3076
  287.0 249.2 %copy-start.26 = (s32[16]{0:T(128)S(1)}, s32[16]{0:T(128)}, u32[]{:S(2)}) copy-start(s32[16]{0:T(128)} %reshape.328) | copy-start | bytes 196
  287.0 251.1 %copy-start.36 = (pred[2,8]{0,1:T(8,128)(4,1)S(1)}, pred[2,8]{0,1:T(8,128)(4,1)}, u32[]{:S(2)}) copy-start(pred[2,8]{0,1:T(8,128)(4,1)} %copy.287) | copy-start | bytes 52
  287.0 7.7 %copy-start.7 = (bf16[2,4,256,256]{3,2,1,0:T(8,128)(2,1)}, bf16[2,4,256,256]{3,2,1,0:T(8,128)(2,1)S(1)}, u32[]{:S(2)}) copy-start(bf16[2,4,256,256]{3,2,1,0:T(8,128)(2,1)S(1)} %get-tuple-element.586) | copy-start | bytes 3145732 | tf_op jit(solution)/shard_map/vmap()/while
  315.8 5.1 copy-start.1
  315.8 6.2 copy-start.2
  315.8 6.4 copy-start.6
  324.7 4.0 copy-start.3
  328.7 4.5 copy-start.8
  334.2 6.4 copy-start.5
  343.5 5.4 copy-start.10
  348.9 7.7 %copy-start.7 = (bf16[2,4,256,256]{3,2,1,0:T(8,128)(2,1)}, bf16[2,4,256,256]{3,2,1,0:T(8,128)(2,1)S(1)}, u32[]{:S(2)}) copy-start(bf16[2,4,256,256]{3,2,1,0:T(8,128)(2,1)S(1)} %get-tuple-element.586) | copy-start | bytes 3145732 | tf_op jit(solution)/shard_map/vmap()/while
  377.7 5.1 copy-start.1
  377.7 6.2 copy-start.2
  377.7 6.4 copy-start.6
  390.5 4.5 copy-start.8
  395.9 6.4 copy-start.5
  405.2 6.1 copy-start.10
  411.3 7.7 %copy-start.7 = (bf16[2,4,256,256]{3,2,1,0:T(8,128)(2,1)}, bf16[2,4,256,256]{3,2,1,0:T(8,128)(2,1)S(1)}, u32[]{:S(2)}) copy-start(bf16[2,4,256,256]{3,2,1,0:T(8,128)(2,1)S(1)} %get-tuple-element.586) | copy-start | bytes 3145732 | tf_op jit(solution)/shard_map/vmap()/while
  440.1 5.1 copy-start.1
  440.1 6.2 copy-start.2
  440.1 6.4 copy-start.6
  452.9 4.5 copy-start.8
  458.4 6.4 copy-start.5
  467.6 6.1 copy-start.10
  473.7 7.7 %copy-start.7 = (bf16[2,4,256,256]{3,2,1,0:T(8,128)(2,1)}, bf16[2,4,256,256]{3,2,1,0:T(8,128)(2,1)S(1)}, u32[]{:S(2)}) copy-start(bf16[2,4,256,256]{3,2,1,0:T(8,128)(2,1)S(1)} %get-tuple-element.586) | copy-start | bytes 3145732 | tf_op jit(solution)/shard_map/vmap()/while
  502.5 5.1 copy-start.1
  502.5 6.2 copy-start.2
  502.5 6.4 copy-start.6
  515.4 4.5 copy-start.8
  520.8 6.4 copy-start.5
  530.1 6.1 copy-start.10
  548.4 9.8 %all-to-all-start.3 = ((f32[2,8,256]{2,0,1:T(2,128)}), f32[2,8,256]{2,0,1:T(2,128)S(1)}, u32[]{:S(2)}, u32[]{:S(2)}) async-start(f32[2,8,256]{2,0,1:T(2,128)} %get-tuple-element.371), calls=%async_computation.3 | async-start | bytes 32768 | tf_op jit(solution)/shard_map/all_to_all | solution.py:328
  558.3 10.9 %all-to-all-start.5 = ((f32[2,8,256]{2,0,1:T(2,128)}), f32[2,8,256]{2,0,1:T(2,128)S(1)}, u32[]{:S(2)}, u32[]{:S(2)}) async-start(f32[2,8,256]{2,0,1:T(2,128)} %get-tuple-element.370), calls=%async_computation.5 | async-start | bytes 32768 | tf_op jit(solution)/shard_map/all_to_all | solution.py:329
  562.5 37.2 %copy-start.16 = (f32[2,4,256,256]{2,3,1,0:T(8,128)S(1)}, f32[2,4,256,256]{2,3,1,0:T(8,128)}, u32[]{:S(2)}) copy-start(f32[2,4,256,256]{2,3,1,0:T(8,128)} %get-tuple-element.120) | copy-start | bytes 6291460
  595.9 5.6 copy-start.31
  595.9 5.6 copy-start.33
  595.9 47.1 %all-to-all-start.4 = ((bf16[2,8,256,128]{3,2,0,1:T(8,128)(2,1)}), bf16[2,8,256,128]{3,2,0,1:T(8,128)(2,1)S(1)}, u32[]{:S(2)}, u32[]{:S(2)}) async-start(bf16[2,8,256,128]{3,2,0,1:T(8,128)(2,1)} %get-tuple-element.374), calls=%async_computation.4 | async-start | bytes 2097152 | tf_op jit(solution)/shard_map/all_to_all | solution.py:322
  599.7 118.3 %all-reduce.4.cloned.1.call-start = ((), (), s32[]{:S(2)}) async-start(), calls=%async_computation.7 | async-start | bytes 4194304 | tf_op jit(solution)/shard_map/psum | solution.py:340
  601.7 4.6 copy-start.23
  606.3 4.4 copy-start.37
  606.3 35.0 %copy-start.22 = (bf16[2,8,256,128]{3,2,0,1:T(8,128)(2,1)S(1)}, bf16[2,8,256,128]{3,2,0,1:T(8,128)(2,1)}, u32[]{:S(2)}) copy-start(bf16[2,8,256,128]{3,2,0,1:T(8,128)(2,1)} %all_to_all.31) | copy-start | bytes 3145732
  654.0 63.9 %copy-start.29 = (s32[2,4]{1,0:T(2,128)S(1)}, s32[2,4]{1,0:T(2,128)}, u32[]{:S(2)}) copy-start(s32[2,4]{1,0:T(2,128)} %get-tuple-element.351) | copy-start | bytes 100
  654.0 63.9 %copy-start.35 = (pred[2,4]{1,0:T(4,128)(4,1)S(1)}, pred[2,4]{1,0:T(4,128)(4,1)}, u32[]{:S(2)}) copy-start(pred[2,4]{1,0:T(4,128)(4,1)} %copy-done.34) | copy-start | bytes 28
  (49 other events, 111.7 us)
Sparse Core Ops, SparseCore 0:
  13.7 165.6 all-gather.1
  604.1 113.7 all-reduce.3
